TPU v7x, 512 devices: a whole 4x8x8 slice. The times are simulated.
512 devices in a mesh: dp: 32 (over y_lo, z), mp: 16 (over x, y_hi, core).
Axes of the slice: x: 4, y: 8 (y_hi: 2, y_lo: 4; y = y_hi * 4 + y_lo), z: 8, core: 2. Of those that a mesh axis runs over, the one named last changes fastest.
Arguments:
- queries: bfloat16 [4096, 4096], P('dp', 'mp'), may hold values from -64 to 64
- database: bfloat16 [16384, 896], P('dp'), may hold values from -9 to 9
- key_weight: bfloat16 [896, 4096], P(None, 'mp'), may hold values from -1 to 2
- value_weight: bfloat16 [896, 4096], P(None, 'mp'), may hold values from -0.1875 to 0.1875
- out_weight: bfloat16 [4096, 8192], P('mp', 'dp'), may hold values from -0.1875 to 0.1875
- neighbours: int32 [64, 2], P('dp'), may hold values from 0 to 127, as said below
Outputs:
- mixed: bfloat16 [4096, 8192], P('dp', 'mp')
Inputs may be any that keep to these rules, and one draw needn't show every extreme that they name: neighbours[c, n] names block neighbours[c, n] % 4 of database shard neighbours[c, n] // 4; among the 4 neighbours of the spans 2 * i to 2 * i + 1, no two lie in the same shard.
All inputs are finite; a program needn't handle non-finite values.
Results may differ from a plain program's by a relative error of at most 0.018.
Values may be sent and summed in bfloat16 or wider, within the bound.
No kernel may reach another device: no remote copies, remote signals or barrier semaphores. Data moves between devices by JAX's collectives and lax.ppermute only.
A program may use at most 64 MiB of HBM per device.

v0:
```python
import math
import jax
import jax.numpy as jnp
from jax import lax
from jax.sharding import PartitionSpec as P

HEAD_DIM = 128
SPAN = 64
NEIGH = 2
NROW = 128
BLK_DEV = 4


def on_device(queries, database, key_weight, value_weight, out_weight, neighbours):
    shard_count = lax.axis_size("dp")
    span_count = neighbours.shape[0]
    inner_width = key_weight.shape[1]
    enc_width = database.shape[1]
    head_count = inner_width // HEAD_DIM
    flat_ids = neighbours.reshape(-1)
    shard_of = flat_ids // BLK_DEV
    local_of = flat_ids % BLK_DEV
    matches = shard_of[None, :] == jnp.arange(shard_count, dtype=jnp.int32)[:, None]
    wanted = jnp.sum(jnp.where(matches, local_of[None, :], 0), axis=1).reshape(shard_count, 1)
    requested = lax.all_to_all(wanted, "dp", split_axis=0, concat_axis=0, tiled=True)
    stored = database.reshape(BLK_DEV, NROW, enc_width)
    outgoing = stored[requested[:, 0]]
    arrived = lax.all_to_all(outgoing, "dp", split_axis=0, concat_axis=0, tiled=True)
    encoded_rows = arrived[shard_of].reshape(-1, enc_width)
    near_keys = jnp.dot(encoded_rows, key_weight, preferred_element_type=jnp.float32).astype(
        jnp.bfloat16
    )
    near_values = jnp.dot(encoded_rows, value_weight, preferred_element_type=jnp.float32).astype(
        jnp.bfloat16
    )
    key_blocks = near_keys.reshape(span_count, NEIGH * NROW, head_count, HEAD_DIM)
    value_blocks = near_values.reshape(span_count, NEIGH * NROW, head_count, HEAD_DIM)
    query_blocks = queries.reshape(span_count, SPAN, head_count, HEAD_DIM)
    scores = jnp.einsum(
        "cqhd,ckhd->chqk", query_blocks, key_blocks, preferred_element_type=jnp.float32
    )
    scores = scores / math.sqrt(HEAD_DIM)
    weights = jax.nn.softmax(scores, axis=-1).astype(jnp.bfloat16)
    attended = jnp.einsum(
        "chqk,ckhd->cqhd", weights, value_blocks, preferred_element_type=jnp.float32
    )
    attended = attended.astype(jnp.bfloat16).reshape(span_count * SPAN, inner_width)
    partial_terms = jnp.dot(
        attended,
        lax.all_gather(out_weight, "dp", axis=1, tiled=True),
        preferred_element_type=jnp.float32,
    )
    return lax.psum_scatter(
        partial_terms.astype(jnp.bfloat16), "mp", scatter_dimension=1, tiled=True
    )


def solution(mesh):
    in_specs = (
        P("dp", "mp"),
        P("dp", None),
        P(None, "mp"),
        P(None, "mp"),
        P("mp", "dp"),
        P("dp", None),
    )
    out_specs = P("dp", "mp")
    return jax.shard_map(
        on_device, mesh=mesh, in_specs=in_specs, out_specs=out_specs, check_vma=False
    )
```

profile of v0, /device:TPU:1, one launch (start us, length us, event | category | flops | bytes accessed | tf_op | source)
XLA Modules:
  0.0 459.4 jit_solution(4644224904882574688)
XLA Ops:
  6.5 0.0 copy-start
  6.5 0.8 reshape.185
  7.4 0.1 select_reduce_fusion
  7.5 0.1 copy.24
  7.6 23.1 %all_to_all.17 = s32[32,1,1]{2,1,0:T(1,128)S(1)} all-to-all(s32[32,1,1]{2,1,0:T(1,128)S(1)} %copy.24), channel_id=1, replica_groups=mesh['dp'=32,'mp'=16] {'dp'}, dimensions={0} | all-to-all | bytes 256 | tf_op jit(solution)/shard_map/all_to_all | solution.py:25
  30.6 0.7 reduce
  31.3 0.0 copy-done
  31.3 4.4 gather_fusion
  35.7 5.0 %all-to-all-start.1 = ((bf16[32,128,896]{2,1,0:T(8,128)(2,1)}), bf16[32,128,896]{2,1,0:T(8,128)(2,1)}, u32[]{:S(2)}, u32[]{:S(2)}) async-start(bf16[32,128,896]{2,1,0:T(8,128)(2,1)} %gather_fusion), calls=%async_computation.1 | async-start | bytes 14680064 | tf_op jit(solution)/shard_map/all_to_all | solution.py:28
  40.8 0.0 copy-start.3
  40.8 0.0 all-gather.2.cloned.1.call-start
  40.8 0.7 all-gather.2.cloned.1.call-update
  41.5 0.0 reduce-scatter.2.cloned.1.call-start
  41.6 0.0 copy-done.4
  41.6 0.1 reshape.186
  41.7 0.0 copy-done.1
  41.7 221.5 %all-to-all-done.1 = bf16[32,128,896]{2,1,0:T(8,128)(2,1)} async-done(((bf16[32,128,896]{2,1,0:T(8,128)(2,1)}), bf16[32,128,896]{2,1,0:T(8,128)(2,1)}, u32[]{:S(2)}, u32[]{:S(2)}) %all-to-all-start.1) | async-done | bytes 7340064 | tf_op jit(solution)/shard_map/all_to_all | solution.py:28
  263.3 3.8 gather_fusion.1
  267.1 0.0 copy-done.2
  267.1 0.4 convolution_convert_fusion.1
  267.6 0.1 reshape.189
  267.6 0.0 copy-done.3
  267.6 0.4 convolution_convert_fusion.2
  268.1 0.1 reshape.188
  268.1 0.2 fusion.2
  268.4 0.2 fusion.14
  268.6 0.5 fusion.4
  269.1 0.1 copy.28
  269.2 58.5 %all-gather.2.cloned.1.call-done = bf16[256,8192]{1,0:T(8,128)(2,1)} async-done(((bf16[256,256]{1,0:T(8,128)(2,1)}), bf16[256,8192]{1,0:T(8,128)(2,1)}) %all-gather.2.cloned.1.call-update) | async-done | bytes 4194320 | tf_op jit(solution)/shard_map/all_gather | solution.py:50
  327.7 4.3 convolution_convert_fusion
  331.9 0.0 reduce-scatter.2.cloned.1.call-update
  332.0 120.6 %reduce-scatter.2.cloned.1.call-done = bf16[128,512]{1,0:T(8,128)(2,1)} async-done(((bf16[128,8192]{1,0:T(8,128)(2,1)}), bf16[128,512]{1,0:T(8,128)(2,1)}) %reduce-scatter.2.cloned.1.call-update) | async-done | bytes 131088 | tf_op jit(solution)/shard_map/reduce_scatter | solution.py:53
  (9 shorter events, 0.1 us)
Async XLA Ops:
  6.5 24.8 %copy-start = (bf16[512,896]{1,0:T(8,128)(2,1)S(1)}, bf16[512,896]{1,0:T(8,128)(2,1)}, u32[]{:S(2)}) copy-start(bf16[512,896]{1,0:T(8,128)(2,1)} %param.7) | copy-start | bytes 2752516
  35.7 5.9 %copy-start.4 = (s32[2,2]{1,0:T(2,128)S(1)}, s32[2,2]{1,0:T(2,128)}, u32[]{:S(2)}) copy-start(s32[2,2]{1,0:T(2,128)} %param.11) | copy-start | bytes 52
  35.7 5.9 %copy-start.1 = (bf16[128,256]{1,0:T(8,128)(2,1)S(1)}, bf16[128,256]{1,0:T(8,128)(2,1)}, u32[]{:S(2)}) copy-start(bf16[128,256]{1,0:T(8,128)(2,1)} %param.6) | copy-start | bytes 196612
  35.7 231.4 %copy-start.2 = (bf16[896,256]{1,0:T(8,128)(2,1)S(1)}, bf16[896,256]{1,0:T(8,128)(2,1)}, u32[]{:S(2)}) copy-start(bf16[896,256]{1,0:T(8,128)(2,1)} %param.8) | copy-start | bytes 1376260
  35.7 227.5 %all-to-all-start.1 = ((bf16[32,128,896]{2,1,0:T(8,128)(2,1)}), bf16[32,128,896]{2,1,0:T(8,128)(2,1)}, u32[]{:S(2)}, u32[]{:S(2)}) async-start(bf16[32,128,896]{2,1,0:T(8,128)(2,1)} %gather_fusion), calls=%async_computation.1 | async-start | bytes 14680064 | tf_op jit(solution)/shard_map/all_to_all | solution.py:28
  40.8 226.8 %copy-start.3 = (bf16[896,256]{1,0:T(8,128)(2,1)S(1)}, bf16[896,256]{1,0:T(8,128)(2,1)}, u32[]{:S(2)}) copy-start(bf16[896,256]{1,0:T(8,128)(2,1)} %param.9) | copy-start | bytes 1376260
  40.8 286.9 %all-gather.2.cloned.1.call-start = ((), (), s32[]{:S(2)}) async-start(), calls=%async_computation.3 | async-start | bytes 4325376 | tf_op jit(solution)/shard_map/all_gather | solution.py:50
  41.5 411.1 %reduce-scatter.2.cloned.1.call-start = ((), (), s32[]{:S(2)}) async-start(), calls=%async_computation.4 | async-start | bytes 2228224 | tf_op jit(solution)/shard_map/reduce_scatter | solution.py:53
Sparse Core Ops, SparseCore 0:
  43.6 283.9 all-gather.1
  332.5 120.0 reduce-scatter.1
where the time goes:
time: 460 us; the launch traced here: 459 us
  waiting for transfers between devices  401 us (87%)
  blocking collectives  23.1 us (5%)
  between operations  13.5 us (3%)
  local copies, waits for them, and re-layouts  9.5 us (2%)
  matrix products  5.86 us (1%)
  starting transfers between devices  5.12 us (1%)
    all_to_all x1, waiting for transfers between devices, on_device(): lax.all_to_all(outgoing, 'dp', split_axis=0, concat_axis=0, tiled=True)  222 us
    reduce_scatter x1, waiting for transfers between devices, on_device(): lax.psum_scatter(partial_terms.astype(jnp.bfloat16), 'mp', scatter_dimens...  121 us
    all_gather x1, waiting for transfers between devices, on_device(): lax.all_gather(out_weight, 'dp', axis=1, tiled=True)  58.5 us
    all_to_all x1, blocking collectives, on_device(): lax.all_to_all(wanted, 'dp', split_axis=0, concat_axis=0, tiled=True)  23.1 us
  transfers between devices with their start and end apart: 3, of which 3 were waited for; matrix products, arithmetic and copies ran while one was open for 1% of the time, Pallas kernels for 0%

commit v1 on v0

--- a/solution.py
+++ b/solution.py
@@ -45,11 +45,10 @@
         "chqk,ckhd->cqhd", weights, value_blocks, preferred_element_type=jnp.float32
     )
     attended = attended.astype(jnp.bfloat16).reshape(span_count * SPAN, inner_width)
-    partial_terms = jnp.dot(
-        attended,
-        lax.all_gather(out_weight, "dp", axis=1, tiled=True),
-        preferred_element_type=jnp.float32,
+    cards_pair = lambda raw: jnp.concatenate(
+        lax.all_to_all(jnp.stack([raw for _ in range(lax.axis_size("dp"))]), "dp", 0, 0), axis=1
     )
+    partial_terms = jnp.dot(attended, cards_pair(out_weight), preferred_element_type=jnp.float32)
     return lax.psum_scatter(
         partial_terms.astype(jnp.bfloat16), "mp", scatter_dimension=1, tiled=True
     )

time: 460 us -> 528 us (1.15)
  waiting for transfers between devices: 401 us -> 438 us
  starting transfers between devices: 5.12 us -> 33.9 us
    all_to_all x0 -> x1, waiting for transfers between devices: none -> 96.6 us  [on_device(): lax.all_to_all(jnp.stack([raw for _ in range(lax.axis_size('dp'))]), 'dp'...]
    all_gather x1 -> x0, waiting for transfers between devices: 58.5 us -> none  [on_device(): lax.all_gather(out_weight, 'dp', axis=1, tiled=True)]
    all_to_all x0 -> x1, starting transfers between devices: none -> 28.8 us  [on_device(): lax.all_to_all(jnp.stack([raw for _ in range(lax.axis_size('dp'))]), 'dp'...]
    all_to_all x1, waiting for transfers between devices: 222 us -> 200 us  [on_device(): lax.all_to_all(outgoing, 'dp', split_axis=0, concat_axis=0, tiled=True)]
    reduce_scatter x1, waiting for transfers between devices: 121 us -> 141 us  [on_device(): lax.psum_scatter(partial_terms.astype(jnp.bfloat16), 'mp', scatter_dimens...]
where the time goes in v1:
time: 528 us
  waiting for transfers between devices  438 us (83%)
  starting transfers between devices  33.9 us (6%)
  blocking collectives  23.1 us (4%)
  between operations  13.6 us (3%)
  local copies, waits for them, and re-layouts  12.1 us (2%)
  matrix products  6.62 us (1%)
    all_to_all x1, waiting for transfers between devices, on_device(): lax.all_to_all(outgoing, 'dp', split_axis=0, concat_axis=0, tiled=True)  200 us
    reduce_scatter x1, waiting for transfers between devices, on_device(): lax.psum_scatter(partial_terms.astype(jnp.bfloat16), 'mp', scatter_dimens...  141 us
    all_to_all x1, waiting for transfers between devices, on_device(): lax.all_to_all(jnp.stack([raw for _ in range(lax.axis_size('dp'))]), 'dp'...  96.6 us
    all_to_all x1, starting transfers between devices, on_device(): lax.all_to_all(jnp.stack([raw for _ in range(lax.axis_size('dp'))]), 'dp'...  28.8 us
    all_to_all x1, blocking collectives, on_device(): lax.all_to_all(wanted, 'dp', split_axis=0, concat_axis=0, tiled=True)  23.1 us
  transfers between devices with their start and end apart: 3, of which 3 were waited for; matrix products, arithmetic and copies ran while one was open for 1% of the time, Pallas kernels for 0%

profile of v1, /device:TPU:1, one launch (start us, length us, event | category | flops | bytes accessed | tf_op | source)
XLA Modules:
  0.0 527.9 jit_solution(14895714873590767199)
XLA Ops:
  6.5 0.0 copy-start
  6.5 0.8 reshape.193
  7.4 0.1 select_reduce_fusion
  7.5 0.1 copy.27
  7.6 23.1 %all_to_all.22 = s32[32,1,1]{2,1,0:T(1,128)S(1)} all-to-all(s32[32,1,1]{2,1,0:T(1,128)S(1)} %copy.27), channel_id=1, replica_groups=mesh['dp'=32,'mp'=16] {'dp'}, dimensions={0} | all-to-all | bytes 256 | tf_op jit(solution)/shard_map/all_to_all | solution.py:25
  30.6 0.7 reduce
  31.3 0.0 copy-done
  31.3 4.4 gather_fusion
  35.7 5.0 all-to-all-start.1
  40.8 0.0 copy-done.1
  40.8 0.1 copy.32
  40.9 200.3 %all-to-all-done.1 = bf16[32,128,896]{2,1,0:T(8,128)(2,1)} async-done(((bf16[32,128,896]{2,1,0:T(8,128)(2,1)}), bf16[32,128,896]{2,1,0:T(8,128)(2,1)}, u32[]{:S(2)}, u32[]{:S(2)}) %all-to-all-start.1) | async-done | bytes 7340064 | tf_op jit(solution)/shard_map/all_to_all | solution.py:28
  241.2 2.5 stack.2
  243.7 28.8 %all-to-all-start.2 = ((bf16[32,256,256]{1,2,0:T(8,128)(2,1)}), bf16[32,256,256]{1,2,0:T(8,128)(2,1)}, u32[]{:S(2)}, u32[]{:S(2)}) async-start(bf16[32,256,256]{1,2,0:T(8,128)(2,1)} %stack.2), calls=%async_computation.2 | async-start | bytes 8388608 | tf_op jit(solution)/shard_map/all_to_all | solution.py:49
  272.5 0.0 reduce-scatter.2.cloned.1.call-start
  272.6 0.0 copy-done.5
  272.6 0.1 reshape.194
  272.7 0.0 copy-done.2
  272.7 3.8 gather_fusion.1
  276.5 0.0 copy-done.3
  276.5 0.4 convolution_convert_fusion.1
  277.0 0.1 reshape.197
  277.1 0.4 convolution_convert_fusion.2
  277.5 0.1 reshape.196
  277.6 0.2 fusion.2
  277.8 0.2 fusion.14
  278.0 0.5 fusion.4
  278.5 0.1 copy.31
  278.6 96.6 %all-to-all-done.2 = bf16[32,256,256]{1,2,0:T(8,128)(2,1)} async-done(((bf16[32,256,256]{1,2,0:T(8,128)(2,1)}), bf16[32,256,256]{1,2,0:T(8,128)(2,1)}, u32[]{:S(2)}, u32[]{:S(2)}) %all-to-all-start.2) | async-done | bytes 4194336 | tf_op jit(solution)/shard_map/all_to_all | solution.py:49
  375.2 5.0 convolution_convert_fusion
  380.2 0.0 reduce-scatter.2.cloned.1.call-update
  380.3 140.8 %reduce-scatter.2.cloned.1.call-done = bf16[128,512]{1,0:T(8,128)(2,1)} async-done(((bf16[128,8192]{1,0:T(8,128)(2,1)}), bf16[128,512]{1,0:T(8,128)(2,1)}) %reduce-scatter.2.cloned.1.call-update) | async-done | bytes 131088 | tf_op jit(solution)/shard_map/reduce_scatter | solution.py:52
  (12 shorter events, 0.1 us)
Async XLA Ops:
  6.5 24.8 %copy-start = (bf16[512,896]{1,0:T(8,128)(2,1)S(1)}, bf16[512,896]{1,0:T(8,128)(2,1)}, u32[]{:S(2)}) copy-start(bf16[512,896]{1,0:T(8,128)(2,1)} %param.7) | copy-start | bytes 2752516
  35.7 5.1 copy-start.1
  35.7 205.5 %all-to-all-start.1 = ((bf16[32,128,896]{2,1,0:T(8,128)(2,1)}), bf16[32,128,896]{2,1,0:T(8,128)(2,1)}, u32[]{:S(2)}, u32[]{:S(2)}) async-start(bf16[32,128,896]{2,1,0:T(8,128)(2,1)} %gather_fusion), calls=%async_computation.1 | async-start | bytes 14680064 | tf_op jit(solution)/shard_map/all_to_all | solution.py:28
  243.7 28.9 %copy-start.5 = (s32[2,2]{1,0:T(2,128)S(1)}, s32[2,2]{1,0:T(2,128)}, u32[]{:S(2)}) copy-start(s32[2,2]{1,0:T(2,128)} %param.11) | copy-start | bytes 52
  243.7 29.0 %copy-start.2 = (bf16[128,256]{1,0:T(8,128)(2,1)S(1)}, bf16[128,256]{1,0:T(8,128)(2,1)}, u32[]{:S(2)}) copy-start(bf16[128,256]{1,0:T(8,128)(2,1)} %param.6) | copy-start | bytes 196612
  243.7 32.8 %copy-start.3 = (bf16[896,256]{1,0:T(8,128)(2,1)S(1)}, bf16[896,256]{1,0:T(8,128)(2,1)}, u32[]{:S(2)}) copy-start(bf16[896,256]{1,0:T(8,128)(2,1)} %param.8) | copy-start | bytes 1376260
  243.7 33.3 %copy-start.4 = (bf16[896,256]{1,0:T(8,128)(2,1)S(1)}, bf16[896,256]{1,0:T(8,128)(2,1)}, u32[]{:S(2)}) copy-start(bf16[896,256]{1,0:T(8,128)(2,1)} %param.9) | copy-start | bytes 1376260
  243.7 131.5 %all-to-all-start.2 = ((bf16[32,256,256]{1,2,0:T(8,128)(2,1)}), bf16[32,256,256]{1,2,0:T(8,128)(2,1)}, u32[]{:S(2)}, u32[]{:S(2)}) async-start(bf16[32,256,256]{1,2,0:T(8,128)(2,1)} %stack.2), calls=%async_computation.2 | async-start | bytes 8388608 | tf_op jit(solution)/shard_map/all_to_all | solution.py:49
  272.5 248.5 %reduce-scatter.2.cloned.1.call-start = ((), (), s32[]{:S(2)}) async-start(), calls=%async_computation.4 | async-start | bytes 2228224 | tf_op jit(solution)/shard_map/reduce_scatter | solution.py:52
Sparse Core Ops, SparseCore 0:
  380.4 140.6 reduce-scatter.1
